TPU v7x, 128 devices: a whole 4x4x4 slice. The times are simulated.
128 devices in a mesh: seq: 32 (over z, y, core), tp: 4 (over x).
Axes of the slice: x: 4, y: 4, z: 4, core: 2. Of those that a mesh axis runs over, the one named last changes fastest.
Arguments:
- tokens: bfloat16 [32768, 2048], P('seq', 'tp'), may hold values from -8 to 8
- col_order: int32 [32768], P('seq'), may hold values from 0 to 32767, as said below
- in_gain: float32 [2, 2048], replicated, may hold values from 0.5 to 1.5
- w_in: bfloat16 [2, 2048, 2, 2048], P(None, None, None, 'tp'), may hold values from -0.125 to 0.125
- w_bc: bfloat16 [2, 2048, 256], replicated, may hold values from -0.0625 to 0.0625
- w_dt: bfloat16 [2, 2048, 32], P(None, None, 'tp'), may hold values from -2 to 2
- conv_x: float32 [2, 4, 2048], P(None, None, 'tp'), may hold values from -3 to 3
- conv_bc: float32 [2, 4, 256], replicated, may hold values from -3 to 3
- dt_bias: float32 [2, 32], P(None, 'tp'), may hold values from -1 to 0.5
- a_log: float32 [2, 32], P(None, 'tp'), may hold values from -16 to -2, as said below
- d_skip: float32 [2, 32], P(None, 'tp'), may hold values from 0.5 to 2
- out_gain: float32 [2, 2048], P(None, 'tp'), may hold values from 0.5 to 1.5
- w_out: bfloat16 [2, 2048, 2048], P(None, 'tp'), may hold values from -0.125 to 0.125
Outputs:
- mixed_out: bfloat16 [32768, 2048], P('seq', 'tp')
Inputs may be any that keep to these rules, and one draw needn't show every extreme that they name: `col_order`: A permutation of the 32768 positions of a frame of 64 rows and 512 columns stored row by row: the column order visits the columns one after another in a drawn order, each from top to bottom or from bottom to top as drawn. So every aligned block of 1024 positions takes exactly 32 row-order positions from each aligned block of 1024 row-order positions. Each head's decay rate exp(a_log) is either between about one in fifty and one in seventeen a step or between 0.3 / 32768 and 2 / 32768 a step.
All inputs are finite; a program needn't handle non-finite values.
Results may differ from a plain program's by a relative error of at most 0.024.
Values may be sent and summed in bfloat16 or wider, within the bound.
No kernel may reach another device: no remote copies, remote signals or barrier semaphores. Data moves between devices by JAX's collectives and lax.ppermute only.
A program may use at most 128 MiB of HBM per device.

v0:
```python
import jax
import jax.numpy as jnp
from jax import lax
from jax.sharding import Mesh
from jax.sharding import PartitionSpec as P

HEAD_DIM = 64
STATE = 128
STRETCH = 128
SEQ = ("seq_0", "seq_1", "seq_2")
highest = lax.Precision.HIGHEST
epsilon = 1e-05


def laid_out(blocks, dim):
    blocks = jnp.moveaxis(blocks, 0, dim)
    lengths = blocks.shape
    return blocks.reshape(*lengths[:dim], lengths[dim] * lengths[dim + 1], *lengths[dim + 2 :])


def sent_to_all(x, axis):
    devices = lax.axis_size(axis)
    return lax.all_to_all(jnp.broadcast_to(x[None], (devices, *x.shape)), axis, 0, 0, tiled=True)


def gathered_copies(x, axis, dim):
    return laid_out(sent_to_all(x, axis), dim)


def passed_along(x, axis, by):
    devices = lax.axis_size(axis)
    pairs = [(i, i + by) for i in range(devices) if 0 <= i + by < devices]
    return lax.ppermute(x, axis, pairs)


def in_blocks(x, dim, devices):
    lengths = x.shape
    blocks = x.reshape(*lengths[:dim], devices, lengths[dim] // devices, *lengths[dim + 1 :])
    return jnp.moveaxis(blocks, dim, 0)


def moved_by_axis(blocks, axes, turns):
    lengths = [lax.axis_size(a) for a in axes]
    blocks = blocks.reshape(*lengths, *blocks.shape[1:])
    for k in turns:
        blocks = lax.all_to_all(blocks, axes[k], split_axis=k, concat_axis=k, tiled=True)
    return blocks.reshape(-1, *blocks.shape[len(axes) :])


def exchange_by_chip(x, groups, turns, split_dim, concat_dim):
    devices = lax.axis_size(groups[0]) * lax.axis_size(groups[1])
    blocks = in_blocks(x, split_dim, devices)
    return laid_out(moved_by_axis(blocks, groups, turns), concat_dim)


def causal_mix(current, rim, taps):
    length = current.shape[0]
    extended = jnp.concatenate([rim, current], axis=0).astype(jnp.float32)
    mixed = jnp.zeros(current.shape, jnp.float32)
    for offset in range(taps.shape[0]):
        mixed = mixed + taps[offset] * extended[offset : offset + length]
    return mixed


def advance(state, pieces):
    factor, fresh = pieces
    return (factor[:, None, None] * state + fresh, state)


def incoming_state(local_end, device_log):
    count = lax.axis_size(SEQ)
    own_index = lax.axis_index(SEQ)
    gathered = gathered_copies(device_log, SEQ, 0).reshape(count, device_log.shape[0])
    before = jnp.cumsum(gathered, axis=0) - gathered
    earlier = (jnp.arange(count) < own_index)[:, None]
    own_prefix = jnp.sum(jnp.where(earlier, gathered, 0.0), axis=0)
    spans = jnp.where(earlier, own_prefix[None, :] - before - gathered, -jnp.inf)
    factors = jnp.exp(spans)
    return jnp.zeros(local_end.shape, jnp.float32) + jnp.einsum(
        "mh,mhpn->hpn",
        factors,
        lax.all_gather(local_end[None].astype(jnp.bfloat16), SEQ, axis=0, tiled=True).astype(
            jnp.float32
        ),
        precision=highest,
    )


def mixer(full, which, params):
    in_gain, w_in, w_bc, w_dt, conv_x, conv_bc, dt_bias, a_log, d_skip, out_gain, w_out = params
    row_count, model_width = full.shape
    inner = w_in.shape[3]
    head_count = inner // HEAD_DIM
    lag = conv_x.shape[1] - 1
    widen = full.astype(jnp.float32)
    scale = lax.rsqrt(jnp.mean(widen * widen, axis=-1, keepdims=True) + epsilon)
    normed = (widen * scale * in_gain[which]).astype(jnp.bfloat16)
    projected = jnp.dot(
        normed, w_in[which].reshape(model_width, 2 * inner), preferred_element_type=jnp.float32
    )
    pre_x = projected[:, :inner].astype(jnp.bfloat16)
    gate_z = projected[:, inner:].astype(jnp.bfloat16)
    pre_bc = jnp.dot(normed, w_bc[which], preferred_element_type=jnp.float32).astype(jnp.bfloat16)
    dt_raw = jnp.dot(normed, w_dt[which], preferred_element_type=jnp.float32)
    rim_x, rim_bc = passed_along((pre_x[row_count - lag :], pre_bc[row_count - lag :]), SEQ, 1)
    conv_out = jax.nn.silu(causal_mix(pre_x, rim_x, conv_x[which]))
    bc_out = jax.nn.silu(causal_mix(pre_bc, rim_bc, conv_bc[which]))
    step_size = jax.nn.softplus(dt_raw + dt_bias[which])
    decay_log = -step_size * jnp.exp(a_log[which])
    heads_in = conv_out.reshape(row_count, head_count, HEAD_DIM)
    feed = heads_in * step_size[:, :, None]
    blocks = row_count // STRETCH
    log_blocks = decay_log.reshape(blocks, STRETCH, head_count)
    b_blocks = bc_out[:, :STATE].reshape(blocks, STRETCH, STATE)
    c_blocks = bc_out[:, STATE:].reshape(blocks, STRETCH, STATE)
    feed_blocks = feed.reshape(blocks, STRETCH, head_count, HEAD_DIM)
    cumul = jnp.cumsum(log_blocks, axis=1)
    cumul_t = jnp.transpose(cumul, (0, 2, 1))
    lower = jnp.arange(STRETCH)[:, None] >= jnp.arange(STRETCH)[None, :]
    spread = jnp.where(lower[None, None], cumul_t[..., :, None] - cumul_t[..., None, :], -jnp.inf)
    intersection = jnp.einsum("cqn,ckn->cqk", c_blocks, b_blocks, precision=highest)
    inside = jnp.einsum(
        "chqk,ckhp->cqhp", intersection[:, None] * jnp.exp(spread), feed_blocks, precision=highest
    )
    to_end = jnp.exp(cumul_t[..., -1:] - cumul_t)
    fresh = jnp.einsum("chk,ckn,ckhp->chpn", to_end, b_blocks, feed_blocks, precision=highest)
    block_decay = jnp.exp(cumul_t[..., -1])
    start_state = jnp.zeros((head_count, HEAD_DIM, STATE), jnp.float32)
    local_end, entering = lax.scan(advance, start_state, (block_decay, fresh))
    carried = (
        jnp.einsum("cqn,chpn->cqhp", c_blocks, entering, precision=highest)
        * jnp.exp(cumul)[..., None]
    )
    block_sums = cumul[:, -1, :]
    prior = jnp.cumsum(block_sums, axis=0) - block_sums
    device_cumul = cumul + prior[:, None, :]
    device_log = jnp.sum(block_sums, axis=0)
    arriving = incoming_state(local_end, device_log)
    correction = (
        jnp.einsum("cqn,hpn->cqhp", c_blocks, arriving, precision=highest)
        * jnp.exp(device_cumul)[..., None]
    )
    ssd = (inside + carried + correction).reshape(row_count, head_count, HEAD_DIM) + d_skip[which][
        None, :, None
    ] * heads_in
    gated = ssd * jax.nn.silu(gate_z.astype(jnp.float32).reshape(row_count, head_count, HEAD_DIM))
    norm_scale = lax.rsqrt(jnp.mean(gated * gated, axis=-1, keepdims=True) + epsilon)
    mixed_heads = (
        (gated * norm_scale * out_gain[which].reshape(head_count, HEAD_DIM))
        .reshape(row_count, inner)
        .astype(jnp.bfloat16)
    )
    return jnp.dot(mixed_heads, w_out[which], preferred_element_type=jnp.float32)


def spread_features(piece):
    return lax.all_gather(piece, "tp", axis=1, tiled=True)


def collect_heads(partial_sum):
    return lax.psum_scatter(
        partial_sum.astype(jnp.bfloat16), "tp", scatter_dimension=1, tiled=True
    ).astype(jnp.float32)


def reorder_rows(stream, col_order):
    count = lax.axis_size(SEQ)
    row_count = stream.shape[0]
    block_rows = row_count // count
    source = col_order // row_count
    local_index = col_order % row_count
    grouping = jnp.argsort(source, stable=True)
    wanted = local_index[grouping].reshape(count, block_rows)
    asked = exchange_by_chip(wanted, (("seq_0", "seq_1"), "seq_2"), (1, 0), 0, 0)
    payload = stream[asked.reshape(-1)].reshape(count, block_rows, stream.shape[1])
    arrived = exchange_by_chip(payload, (("seq_0", "seq_1"), "seq_2"), (1, 0), 0, 0).reshape(
        row_count, stream.shape[1]
    )
    placement = jnp.argsort(grouping)
    return arrived[placement]


def body(
    tokens,
    col_order,
    in_gain,
    w_in,
    w_bc,
    w_dt,
    conv_x,
    conv_bc,
    dt_bias,
    a_log,
    d_skip,
    out_gain,
    w_out,
):
    params = (in_gain, w_in, w_bc, w_dt, conv_x, conv_bc, dt_bias, a_log, d_skip, out_gain, w_out)
    first_full = spread_features(tokens)
    first_part = mixer(first_full, 0, params)
    row_result = (tokens.astype(jnp.float32) + collect_heads(first_part)).astype(jnp.bfloat16)
    own_rows = reorder_rows(row_result, col_order)
    second_full = spread_features(own_rows)
    second_part = mixer(second_full, 1, params)
    return (own_rows.astype(jnp.float32) + collect_heads(second_part)).astype(jnp.bfloat16)


def solution(mesh):
    torus = Mesh(mesh.devices.reshape(4, 4, 2, mesh.shape["tp"]), ("seq_0", "seq_1", "seq_2", "tp"))
    return jax.shard_map(
        body,
        mesh=torus,
        in_specs=(
            P(SEQ, "tp"),
            P(SEQ),
            P(),
            P(None, None, None, "tp"),
            P(),
            P(None, None, "tp"),
            P(None, None, "tp"),
            P(),
            P(None, "tp"),
            P(None, "tp"),
            P(None, "tp"),
            P(None, "tp"),
            P(None, "tp", None),
        ),
        out_specs=P(SEQ, "tp"),
        check_vma=False,
    )
```

profile of v0, /device:TPU:1, one launch (start us, length us, event | category | flops | bytes accessed | tf_op | source)
XLA Modules:
  0.0 575.8 jit_solution(12658820675319592210)
XLA Ops:
  7.3 7.9 %fusion.98 = (bf16[1,2048,2,512]{3,2,1,0:T(2,128)(2,1)}, bf16[1,2048,2,512]{3,2,1,0:T(2,128)(2,1)S(1)}) fusion(bf16[2,2048,2,512]{3,2,1,0:T(2,128)(2,1)} %param.20), kind=kLoop, calls=%fused_computation.187 | loop fusion | bytes 16777216 | tf_op jit(solution)/shard_map/slice | solution.py:99
  15.3 3.2 copy.200
  20.9 39.6 %all-gather.8.cloned.1.call-done = bf16[1024,2048]{1,0:T(8,128)(2,1)} async-done(((bf16[1024,512]{1,0:T(8,128)(2,1)}), bf16[1024,2048]{1,0:T(8,128)(2,1)}) %all-gather.8.cloned.1.call-update) | async-done | bytes 4194320 | tf_op jit(solution)/shard_map/all_gather | solution.py:157
  60.5 3.2 fusion.2
  63.9 7.2 %convolution_convert_fusion.3 = bf16[1024,1024]{1,0:T(8,128)(2,1)S(1)} fusion(bf16[2048,1024]{1,0:T(8,128)(2,1)} %bitcast.229, bf16[1024,2048]{1,0:T(8,128)(2,1)S(1)} %copy-done.14, f32[2048]{0:T(1024)S(1)} %bitcast.255, f32[1024]{0:T(1024)S(1)} %add_rsqrt_fusion.1), kind=kOutput, calls=%fused_computation.92 | convolution fusion | flops 4304404480 | bytes 10498048 | tf_op jit(solution)/shard_map/dot_general | solution.py:98
  75.0 23.3 %fusion.107 = f32[8,128,8]{2,0,1:T(8,128)S(1)} fusion(f32[8,128,8]{2,0,1:T(8,128)S(1)} %copy.146), kind=kOutput, calls=%fused_computation.197 | output fusion | flops 1040384 | bytes 65536 | tf_op jit(solution)/shard_map/jit(cumsum)/reduce_window_sum | solution.py:117
  98.9 3.7 collective-permute-start
  102.6 3.8 convolution_convert_fusion.5
  107.3 2.1 collective-permute-start.1
  114.8 2.6 divide_multiply_fusion.1
  117.3 2.9 copy.144
  120.3 2.1 copy.201
  124.4 3.5 fusion.43
  129.5 19.8 %while.26 = (s32[]{:T(128)}, f32[8,64,128]{2,1,0:T(8,128)S(1)}, f32[8,8,64,128]{3,2,1,0:T(8,128)}, f32[8,8]{1,0:T(8,128)}, f32[8,8,64,128]{3,2,1,0:T(8,128)}, /*index=5*/s32[]{:T(128)}, s32[]{:T(128)}) while((s32[]{:T(128)}, f32[8,64,128]{2,1,0:T(8,128)S(1)}, f32[8,8,64,128]{3,2,1,0:T(8,128)}, f32[8,8]{1,0:T(8,128)}, ...), condition=%wide.region_3.4_spmd.clone, body=%wide.region_2.3_spmd.clone.sunk | while | flops 262147 | bytes 1311424 | solution.py:129
  153.1 7.8 %all-to-all-start = ((f32[32,1,8]{2,1,0:T(1,128)}), f32[32,1,8]{2,1,0:T(1,128)S(1)}, u32[]{:S(2)}, u32[]{:S(2)}) async-start(f32[32,1,8]{2,1,0:T(1,128)} %broadcast_in_dim.64), calls=%async_computation | async-start | bytes 32768 | tf_op jit(solution)/shard_map/all_to_all | solution.py:23
  164.7 2.4 reshape.291
  167.2 4.1 copy.159
  172.9 3.2 fusion.110
  176.1 9.7 %fusion.17 = f32[8,8,64,128]{3,2,1,0:T(8,128)} fusion(f32[8,128,8,64]{1,0,3,2:T(8,128)S(1)} %copy-done.18, f32[8,8,128]{2,1,0:T(8,128)S(1)} %copy.147, f32[8,128,128]{2,1,0:T(8,128)S(1)} %fusion.109, pred[128,128]{1,0:T(8,128)(4,1)S(1)} %iota_compare_fusion), kind=kOutput, calls=%fused_computation.30 | convolution fusion | flops 808452096 | bytes 4767744 | tf_op jit(solution)/shard_map/chqk,ckhp->cqhp/dot_general | solution.py:122
  185.7 11.7 %all-gather.10.cloned.1.call-done = bf16[256,64,128]{2,1,0:T(8,128)(2,1)} async-done(((bf16[8,64,128]{2,1,0:T(8,128)(2,1)}), bf16[256,64,128]{2,1,0:T(8,128)(2,1)}) %all-gather.10.cloned.1.call-update) | async-done | bytes 4194320 | tf_op jit(solution)/shard_map/all_gather | solution.py:82
  197.4 6.2 %fusion.10 = f32[8,1,64,128]{3,1,2,0:T(1,128)S(1)} fusion(f32[32,8,1,1]{0,2,3,1:T(1,128)S(1)} %copy.184, bf16[32,8,64,128]{3,2,1,0:T(8,128)(2,1)} %bitcast.226), kind=kOutput, calls=%fused_computation.23 | convolution fusion | flops 25165824 | bytes 4457472 | tf_op jit(solution)/shard_map/mh,mhpn->hpn/dot_general | solution.py:79
  203.7 5.1 fusion.42
  208.8 2.8 copy.192
  211.6 4.8 reshape.289
  216.7 1.9 copy.160
  218.6 8.5 %convolution_convert_fusion.1 = bf16[1024,2048]{1,0:T(8,128)(2,1)} fusion(bf16[2,512,2048]{2,1,0:T(8,128)(2,1)} %param.29, f32[1024,512]{1,0:T(8,128)} %copy.160, f32[1024,512]{1,0:T(8,128)} %reshape.289, f32[1024,512]{1,0:T(8,128)} %divide_multiply_fusion.1, f32[512]{0:T(512)S(1)} %bitcast.267, f32[512]{0:T(512)S(1)} %copy-done.39, ...), kind=kOutput, calls=%fused_computation.36 | convolution fusion | flops 2155347968 | bytes 13635584 | tf_op jit(solution)/shard_map/dot_general | solution.py:153
  227.8 4.4 sort.34
  232.2 4.5 gather_fusion
  238.1 3.6 all_to_all.38
  242.5 11.0 %all_to_all.39 = s32[16,2,1,32]{3,2,1,0:T(1,128)S(1)} all-to-all(s32[16,2,1,32]{3,2,1,0:T(1,128)S(1)} %copy.162), channel_id=1, replica_groups=mesh['seq_0'=4,'seq_1'=4,'seq_2'=2,'tp'=4] {'seq_0','seq_1'}, dimensions={0} | all-to-all | bytes 8192 | tf_op jit(solution)/shard_map/all_to_all | solution.py:46
  254.8 18.2 %reduce-scatter.3.cloned.1.call-done = bf16[1024,512]{1,0:T(8,128)(2,1)} async-done(((bf16[1024,2048]{1,0:T(8,128)(2,1)}), bf16[1024,512]{1,0:T(8,128)(2,1)}) %reduce-scatter.3.cloned.1.call-update) | async-done | bytes 1048592 | tf_op jit(solution)/shard_map/reduce_scatter | solution.py:161
  274.5 4.0 gather_fusion.1
  278.6 4.8 all_to_all.40
  284.5 6.7 %all-to-all-start.4 = ((bf16[16,2,1,32,512]{4,3,1,2,0:T(8,128)(2,1)}), bf16[16,2,1,32,512]{4,3,1,2,0:T(8,128)(2,1)S(1)}, u32[]{:S(2)}, u32[]{:S(2)}) async-start(bf16[16,2,1,32,512]{4,3,1,2,0:T(8,128)(2,1)} %copy.164), calls=%async_computation.5 | async-start | bytes 2097152 | tf_op jit(solution)/shard_map/all_to_all | solution.py:46
  291.2 4.4 sort.35
  295.6 11.9 %all-to-all-done.4 = bf16[16,2,1,32,512]{4,3,1,2,0:T(8,128)(2,1)S(1)} async-done(((bf16[16,2,1,32,512]{4,3,1,2,0:T(8,128)(2,1)}), bf16[16,2,1,32,512]{4,3,1,2,0:T(8,128)(2,1)S(1)}, u32[]{:S(2)}, u32[]{:S(2)}) %all-to-all-start.4) | async-done | bytes 1048608 | tf_op jit(solution)/shard_map/all_to_all | solution.py:46
  307.5 5.1 gather_fusion.2
  312.8 5.5 copy.202
  318.4 39.9 %all-gather.12.cloned.1.call-done = bf16[1024,2048]{1,0:T(8,128)(2,1)} async-done(((bf16[1024,512]{1,0:T(8,128)(2,1)}), bf16[1024,2048]{1,0:T(8,128)(2,1)}) %all-gather.12.cloned.1.call-update) | async-done | bytes 4194320 | tf_op jit(solution)/shard_map/all_gather | solution.py:157
  358.3 3.2 fusion.5
  363.7 3.7 collective-permute-start.3
  369.1 23.3 %fusion.108 = f32[8,128,8]{2,0,1:T(8,128)S(1)} fusion(f32[8,128,8]{2,0,1:T(8,128)S(1)} %copy.167), kind=kOutput, calls=%fused_computation.198 | output fusion | flops 1040384 | bytes 65536 | tf_op jit(solution)/shard_map/jit(cumsum)/reduce_window_sum | solution.py:117
  392.5 8.0 %convolution_convert_fusion.2 = bf16[1024,1024]{1,0:T(8,128)(2,1)S(1)} fusion(bf16[2048,1024]{1,0:T(8,128)(2,1)} %bitcast.230, bf16[1024,2048]{1,0:T(8,128)(2,1)} %all-gather.12.cloned.1.call-done, f32[2048]{0:T(1024)S(1)} %bitcast.254, f32[1024]{0:T(1024)S(1)} %add_rsqrt_fusion), kind=kOutput, calls=%fused_computation.91 | convolution fusion | flops 4304404480 | bytes 10498048 | tf_op jit(solution)/shard_map/dot_general | solution.py:98
  403.4 2.1 collective-permute-start.2
  409.2 2.6 divide_multiply_fusion
  411.7 2.9 copy.165
  414.7 2.1 copy.203
  416.7 1.7 broadcast_multiply_fusion
  418.7 3.5 fusion.36
  423.8 19.8 %while.27 = (s32[]{:T(128)}, f32[8,64,128]{2,1,0:T(8,128)S(1)}, f32[8,8,64,128]{3,2,1,0:T(8,128)}, f32[8,8]{1,0:T(8,128)}, f32[8,8,64,128]{3,2,1,0:T(8,128)}, /*index=5*/s32[]{:T(128)}, s32[]{:T(128)}) while((s32[]{:T(128)}, f32[8,64,128]{2,1,0:T(8,128)S(1)}, f32[8,8,64,128]{3,2,1,0:T(8,128)}, f32[8,8]{1,0:T(8,128)}, ...), condition=%wide.region_15.16_spmd.clone, body=%wide.region_14.15_spmd.clone.sunk | while | flops 262147 | bytes 1311424 | solution.py:129
  445.1 7.2 %all-to-all-start.5 = ((f32[32,1,8]{2,1,0:T(1,128)}), f32[32,1,8]{2,1,0:T(1,128)S(1)}, u32[]{:S(2)}, u32[]{:S(2)}) async-start(f32[32,1,8]{2,1,0:T(1,128)} %broadcast_in_dim.112), calls=%async_computation.6 | async-start | bytes 32768 | tf_op jit(solution)/shard_map/all_to_all | solution.py:23
  456.1 2.5 reshape.292
  458.6 4.3 copy.180
  464.5 3.2 fusion.112
  467.7 9.7 %fusion.12 = f32[8,8,64,128]{3,2,1,0:T(8,128)} fusion(f32[8,128,8,64]{1,0,3,2:T(8,128)S(1)} %copy-done.19, f32[8,8,128]{2,1,0:T(8,128)S(1)} %copy.168, f32[8,128,128]{2,1,0:T(8,128)S(1)} %fusion.111, pred[128,128]{1,0:T(8,128)(4,1)S(1)} %iota_compare_fusion), kind=kOutput, calls=%fused_computation.25 | convolution fusion | flops 808452096 | bytes 4767744 | tf_op jit(solution)/shard_map/chqk,ckhp->cqhp/dot_general | solution.py:122
  477.4 13.8 %all-gather.14.cloned.1.call-done = bf16[256,64,128]{2,1,0:T(8,128)(2,1)} async-done(((bf16[8,64,128]{2,1,0:T(8,128)(2,1)}), bf16[256,64,128]{2,1,0:T(8,128)(2,1)}) %all-gather.14.cloned.1.call-update) | async-done | bytes 4194320 | tf_op jit(solution)/shard_map/all_gather | solution.py:82
  491.1 6.0 %fusion.8 = f32[8,1,64,128]{3,1,2,0:T(1,128)S(1)} fusion(f32[32,8,1,1]{0,2,3,1:T(1,128)S(1)} %copy.189, bf16[32,8,64,128]{3,2,1,0:T(8,128)(2,1)} %bitcast.227), kind=kOutput, calls=%fused_computation.21 | convolution fusion | flops 25165824 | bytes 4457472 | tf_op jit(solution)/shard_map/mh,mhpn->hpn/dot_general | solution.py:79
  497.2 5.1 fusion.35
  502.3 2.7 copy.193
  505.0 4.8 reshape.290
  510.1 1.9 copy.181
  512.0 8.4 %convolution_convert_fusion = bf16[1024,2048]{1,0:T(8,128)(2,1)} fusion(bf16[2,512,2048]{2,1,0:T(8,128)(2,1)} %param.29, f32[1024,512]{1,0:T(8,128)} %copy.181, f32[1024,512]{1,0:T(8,128)} %reshape.290, f32[1024,512]{1,0:T(8,128)} %divide_multiply_fusion, f32[512]{0:T(512)S(1)} %bitcast.266, f32[512]{0:T(512)S(1)} %mul.565, bf16[1024,1024]{1,0:T(8,128)(2,1)} %copy-done.17), kind=kOutput, calls=%fused_computation.35 | convolution fusion | flops 2155347968 | bytes 13635584 | tf_op jit(solution)/shard_map/dot_general | solution.py:153
  520.5 45.8 %reduce-scatter.5.cloned.1.call-done = bf16[1024,512]{1,0:T(8,128)(2,1)} async-done(((bf16[1024,2048]{1,0:T(8,128)(2,1)}), bf16[1024,512]{1,0:T(8,128)(2,1)}) %reduce-scatter.5.cloned.1.call-update) | async-done | bytes 1048592 | tf_op jit(solution)/shard_map/reduce_scatter | solution.py:161
  566.3 2.5 add_convert_fusion
  (274 shorter events, 92.6 us)
Async XLA Ops:
  6.5 53.9 %all-gather.8.cloned.1.call-start = ((), (), s32[]{:S(2)}) async-start(), calls=%async_computation.8 | async-start | bytes 5242880 | tf_op jit(solution)/shard_map/all_gather | solution.py:157
  7.3 190.2 %all-gather.10.cloned.1.call-start = ((), (), s32[]{:S(2)}) async-start(), calls=%async_computation.11 | async-start | bytes 4325376 | tf_op jit(solution)/shard_map/all_gather | solution.py:82
  15.3 3.2 copy-start.45
  15.3 3.8 copy-start.46
  15.3 4.4 copy-start.28
  15.3 5.0 copy-start.24
  15.3 5.0 copy-start.25
  60.5 3.4 copy-start.14
  71.1 1.6 copy-start.16
  71.1 2.2 copy-start.50
  98.9 15.1 %collective-permute-start = (bf16[3,512]{1,0:T(4,128)(2,1)}, bf16[3,512]{1,0:T(4,128)(2,1)S(1)}, u32[]{:S(2)}, u32[]{:S(2)}) collective-permute-start(bf16[3,512]{1,0:T(4,128)(2,1)} %slice.314), channel_id=1, source_target_pairs={{0,4},{4,8},{8,12},{12,16},{16,20},{20,24},{24,28},{28,32},{32,36}... | collective-permute-start | bytes 9224 | tf_op jit(solution)/shard_map/ppermute | solution.py:33
  106.4 0.8 copy-start.23
  106.4 5.4 copy-start.34
  106.4 5.4 copy-start.35
  107.3 3.4 collective-permute-start.1
  113.0 1.4 copy-start.12
  122.3 2.0 copy-start.1
  122.3 2.0 copy-start.7
  129.5 20.5 %copy-start.47 = (f32[2,8]{1,0:T(2,128)S(1)}, f32[2,8]{1,0:T(2,128)}, u32[]{:S(2)}) copy-start(f32[2,8]{1,0:T(2,128)} %param.27) | copy-start | bytes 196
  129.5 22.3 %copy-start.37 = (f32[2,512]{1,0:T(2,128)S(1)}, f32[2,512]{1,0:T(2,128)}, u32[]{:S(2)}) copy-start(f32[2,512]{1,0:T(2,128)} %param.28) | copy-start | bytes 12292
  150.5 2.6 copy-start.41
  153.1 18.2 %all-to-all-start = ((f32[32,1,8]{2,1,0:T(1,128)}), f32[32,1,8]{2,1,0:T(1,128)S(1)}, u32[]{:S(2)}, u32[]{:S(2)}) async-start(f32[32,1,8]{2,1,0:T(1,128)} %broadcast_in_dim.64), calls=%async_computation | async-start | bytes 32768 | tf_op jit(solution)/shard_map/all_to_all | solution.py:23
  160.9 112.1 %reduce-scatter.3.cloned.1.call-start = ((), (), s32[]{:S(2)}) async-start(), calls=%async_computation.9 | async-start | bytes 5242880 | tf_op jit(solution)/shard_map/reduce_scatter | solution.py:161
  167.2 4.2 copy-start.26
  167.2 4.5 copy-start.8
  167.2 5.7 copy-start.5
  172.9 3.2 copy-start.18
  197.4 6.3 %copy-start.2 = (f32[64,8,8,128]{3,2,1,0:T(8,128)S(1)}, f32[64,8,8,128]{3,2,1,0:T(8,128)}, u32[]{:S(2)}) copy-start(f32[64,8,8,128]{3,2,1,0:T(8,128)} %copy-done.1) | copy-start | bytes 6291460
  197.4 6.3 %copy-start.21 = (f32[8,128,8,64]{1,3,2,0:T(8,128)S(1)}, f32[8,128,8,64]{1,3,2,0:T(8,128)}, u32[]{:S(2)}) copy-start(f32[8,128,8,64]{1,3,2,0:T(8,128)} %copy.159) | copy-start | bytes 6291460
  197.4 6.3 %copy-start.42 = (f32[8]{0:T(128)S(1)}, f32[8]{0:T(128)}, u32[]{:S(2)}) copy-start(f32[8]{0:T(128)} %copy-done.41) | copy-start | bytes 100
  216.7 1.9 copy-start.39
  216.7 1.9 copy-start.44
  232.2 40.8 %copy-start.11 = (bf16[1024,512]{1,0:T(8,128)(2,1)S(1)}, bf16[1024,512]{1,0:T(8,128)(2,1)}, u32[]{:S(2)}) copy-start(bf16[1024,512]{1,0:T(8,128)(2,1)} %param.17) | copy-start | bytes 3145732
  284.5 23.0 %all-to-all-start.4 = ((bf16[16,2,1,32,512]{4,3,1,2,0:T(8,128)(2,1)}), bf16[16,2,1,32,512]{4,3,1,2,0:T(8,128)(2,1)S(1)}, u32[]{:S(2)}, u32[]{:S(2)}) async-start(bf16[16,2,1,32,512]{4,3,1,2,0:T(8,128)(2,1)} %copy.164), calls=%async_computation.5 | async-start | bytes 2097152 | tf_op jit(solution)/shard_map/all_to_all | solution.py:46
  291.2 67.1 %all-gather.12.cloned.1.call-start = ((), (), s32[]{:S(2)}) async-start(), calls=%async_computation.12 | async-start | bytes 5242880 | tf_op jit(solution)/shard_map/all_gather | solution.py:157
  312.6 178.5 %all-gather.14.cloned.1.call-start = ((), (), s32[]{:S(2)}) async-start(), calls=%async_computation.13 | async-start | bytes 4325376 | tf_op jit(solution)/shard_map/all_gather | solution.py:82
  312.8 48.7 %copy-start.49 = (bf16[2,2048,256]{2,1,0:T(8,128)(2,1)S(1)}, bf16[2,2048,256]{2,1,0:T(8,128)(2,1)}, u32[]{:S(2)}) copy-start(bf16[2,2048,256]{2,1,0:T(8,128)(2,1)} %param.21) | copy-start | bytes 6291460
  318.4 43.2 %copy-start.29 = (f32[1,2048]{1,0:T(1,128)S(1)}, f32[1,2048]{1,0:T(1,128)}, u32[]{:S(2)}) copy-start(f32[1,2048]{1,0:T(1,128)} %get-tuple-element.155) | copy-start | bytes 24580
  358.3 3.4 copy-start.15
  361.8 5.7 copy-start.48
  361.8 5.7 copy-start.51
  363.1 5.7 copy-start.22
  363.7 41.9 %collective-permute-start.3 = (bf16[3,256]{1,0:T(4,128)(2,1)}, bf16[3,256]{1,0:T(4,128)(2,1)}, u32[]{:S(2)}, u32[]{:S(2)}) collective-permute-start(bf16[3,256]{1,0:T(4,128)(2,1)} %slice.336), channel_id=1, source_target_pairs={{0,4},{4,8},{8,12},{12,16},{16,20},{20,24},{24,28},{28,32},{32,36}... | collective-permute-start | bytes 4616 | tf_op jit(solution)/shard_map/ppermute | solution.py:33
  367.4 1.3 copy-start.38
  400.5 2.1 copy-start.17
  402.0 4.7 copy-start.30
  402.0 4.8 copy-start.31
  402.0 4.8 copy-start.32
  402.0 4.8 copy-start.33
  403.4 4.9 collective-permute-start.2
  407.4 1.4 copy-start.13
  416.7 2.0 copy-start.3
  416.7 2.0 copy-start.9
  423.8 20.5 %copy-start.40 = (f32[8]{0:T(128)S(1)}, f32[8]{0:T(128)}, u32[]{:S(2)}) copy-start(f32[8]{0:T(128)} %get-tuple-element.169) | copy-start | bytes 100
  445.1 17.9 %all-to-all-start.5 = ((f32[32,1,8]{2,1,0:T(1,128)}), f32[32,1,8]{2,1,0:T(1,128)S(1)}, u32[]{:S(2)}, u32[]{:S(2)}) async-start(f32[32,1,8]{2,1,0:T(1,128)} %broadcast_in_dim.112), calls=%async_computation.6 | async-start | bytes 32768 | tf_op jit(solution)/shard_map/all_to_all | solution.py:23
  452.3 114.0 %reduce-scatter.5.cloned.1.call-start = ((), (), s32[]{:S(2)}) async-start(), calls=%async_computation.10 | async-start | bytes 5242880 | tf_op jit(solution)/shard_map/reduce_scatter | solution.py:161
  458.6 4.4 copy-start.27
  458.6 4.7 copy-start.10
  458.6 5.9 %copy-start.6 = (f32[8,8,64,128]{3,2,1,0:T(8,128)S(1)}, f32[8,8,64,128]{3,2,1,0:T(8,128)}, u32[]{:S(2)}) copy-start(f32[8,8,64,128]{3,2,1,0:T(8,128)} %get-tuple-element.67) | copy-start | bytes 6291460
  464.5 3.2 copy-start.19
  491.1 6.0 %copy-start.4 = (f32[64,8,8,128]{3,2,1,0:T(8,128)S(1)}, f32[64,8,8,128]{3,2,1,0:T(8,128)}, u32[]{:S(2)}) copy-start(f32[64,8,8,128]{3,2,1,0:T(8,128)} %copy-done.3) | copy-start | bytes 6291460
  491.1 6.0 %copy-start.20 = (f32[8,128,8,64]{1,3,2,0:T(8,128)S(1)}, f32[8,128,8,64]{1,3,2,0:T(8,128)}, u32[]{:S(2)}) copy-start(f32[8,128,8,64]{1,3,2,0:T(8,128)} %copy.180) | copy-start | bytes 6291460
  510.1 1.9 copy-start.43
  520.5 45.9 %copy-start = (bf16[1024,512]{1,0:T(8,128)(2,1)S(1)}, bf16[1024,512]{1,0:T(8,128)(2,1)}, u32[]{:S(2)}) copy-start(bf16[1024,512]{1,0:T(8,128)(2,1)} %gather_fusion.2) | copy-start | bytes 3145732
  (1 other events, 0.7 us)
Sparse Core Ops, SparseCore 0:
  9.0 51.3 all-gather.7
  150.1 47.2 all-gather.9
  227.2 45.7 reduce-scatter.2
  312.7 45.5 all-gather.11
  444.4 46.7 all-gather.13
  520.6 45.6 reduce-scatter.4
where the time goes:
time: 584 us; the launch traced here: 576 us
  waiting for transfers between devices  183 us (31%)
  other arithmetic  118 us (20%)
  local copies, waits for them, and re-layouts  110 us (19%)
  matrix products  97.5 us (17%)
  starting transfers between devices  33.7 us (6%)
  blocking collectives  19.4 us (3%)
  between operations  14.5 us (2%)
    all_gather x2, waiting for transfers between devices, spread_features(): return lax.all_gather(piece, 'tp', axis=1, tiled=True)  79.5 us
    reduce_scatter x2, waiting for transfers between devices, collect_heads(): lax.psum_scatter(partial_sum.astype(jnp.bfloat16), 'tp', scatter_dimensio...  64.1 us
    another operation x2, other arithmetic, mixer(): cumul = jnp.cumsum(log_blocks, axis=1)  46.6 us
    all_gather x2, waiting for transfers between devices, incoming_state(): lax.all_gather(local_end[None].astype(jnp.bfloat16), SEQ, axis=0, tiled=T...  25.5 us
    all_to_all x3, blocking collectives, moved_by_axis(): lax.all_to_all(blocks, axes[k], split_axis=k, concat_axis=k, tiled=True)  19.4 us
    dot_general x2, matrix products, mixer(): jnp.einsum('chqk,ckhp->cqhp', intersection[:, None] * jnp.exp(spread), fe...  19.3 us
    dot_general x2, matrix products, mixer(): jnp.dot(mixed_heads, w_out[which], preferred_element_type=jnp.float32)  17 us
    unnamed x111, local copies, waits for them, and re-layouts  16.7 us
  transfers between devices with their start and end apart: 13, of which 8 were waited for; matrix products, arithmetic and copies ran while one was open for 24% of the time, Pallas kernels for 0%

commit v1 on v0

--- a/solution.py
+++ b/solution.py
@@ -1,8 +1,10 @@
+import functools
 import jax
 import jax.numpy as jnp
 from jax import lax
 from jax.sharding import Mesh
 from jax.sharding import PartitionSpec as P
+from jax.lax import all_to_all, axis_size
 
 HEAD_DIM = 64
 STATE = 128
@@ -10,6 +12,16 @@
 SEQ = ("seq_0", "seq_1", "seq_2")
 highest = lax.Precision.HIGHEST
 epsilon = 1e-05
+
+
+def unite_ratios(xin, named_axis):
+    then = jnp.concatenate(
+        all_to_all(jnp.stack(axis_size(named_axis) * [xin], axis=0), named_axis, 0, 0), axis=0
+    )
+    return then
+
+
+orders_pair = functools.partial(unite_ratios, named_axis=SEQ)
 
 
 def laid_out(blocks, dim):
@@ -79,9 +91,7 @@
     return jnp.zeros(local_end.shape, jnp.float32) + jnp.einsum(
         "mh,mhpn->hpn",
         factors,
-        lax.all_gather(local_end[None].astype(jnp.bfloat16), SEQ, axis=0, tiled=True).astype(
-            jnp.float32
-        ),
+        orders_pair(local_end[None].astype(jnp.bfloat16)).astype(jnp.float32),
         precision=highest,
     )
 

time: 584 us -> 623 us (1.067)
  waiting for transfers between devices: 183 us -> 201 us
  starting transfers between devices: 33.7 us -> 48.2 us
    all_to_all x0 -> x2, waiting for transfers between devices: none -> 46.9 us  [unite_ratios(): all_to_all(jnp.stack(axis_size(named_axis) * [xin], axis=0), named_axis,...]
    all_gather x2 -> x0, waiting for transfers between devices: 25.5 us -> none  [incoming_state(): lax.all_gather(local_end[None].astype(jnp.bfloat16), SEQ, axis=0, tiled=T...]
    all_to_all x0 -> x2, starting transfers between devices: none -> 15.1 us  [unite_ratios(): all_to_all(jnp.stack(axis_size(named_axis) * [xin], axis=0), named_axis,...]
    another operation x2 -> x4, local copies, waits for them, and re-layouts: 3.21 us -> 9.44 us  [the longest x2 6.16 us: unite_ratios(): jnp.stack(axis_size(named_axis) * [xin], axis=0)]
    unnamed x111 -> x127, local copies, waits for them, and re-layouts: 16.7 us -> 17.4 us
  transfers between devices with their start and end apart: 13 -> 13, of which waited for: 8 -> 7; matrix products, arithmetic and copies ran while one was open for 24% -> 27% of each run, Pallas kernels for 0% -> 0%
where the time goes in v1:
time: 623 us; the launch traced here: 614 us
  waiting for transfers between devices  201 us (32%)
  other arithmetic  118 us (19%)
  local copies, waits for them, and re-layouts  112 us (18%)
  matrix products  98.9 us (16%)
  starting transfers between devices  48.2 us (8%)
  blocking collectives  20.7 us (3%)
  between operations  14.3 us (2%)
    all_gather x2, waiting for transfers between devices, spread_features(): return lax.all_gather(piece, 'tp', axis=1, tiled=True)  79.3 us
    reduce_scatter x2, waiting for transfers between devices, collect_heads(): lax.psum_scatter(partial_sum.astype(jnp.bfloat16), 'tp', scatter_dimensio...  62.5 us
    all_to_all x2, waiting for transfers between devices, unite_ratios(): all_to_all(jnp.stack(axis_size(named_axis) * [xin], axis=0), named_axis,...  46.9 us
    another operation x2, other arithmetic, mixer(): cumul = jnp.cumsum(log_blocks, axis=1)  46.6 us
    all_to_all x3, blocking collectives, moved_by_axis(): lax.all_to_all(blocks, axes[k], split_axis=k, concat_axis=k, tiled=True)  20.7 us
    dot_general x2, matrix products, mixer(): jnp.einsum('chqk,ckhp->cqhp', intersection[:, None] * jnp.exp(spread), fe...  19.3 us
    unnamed x127, local copies, waits for them, and re-layouts  17.4 us
    dot_general x2, matrix products, mixer(): jnp.dot(mixed_heads, w_out[which], preferred_element_type=jnp.float32)  17 us
  transfers between devices with their start and end apart: 13, of which 7 were waited for; matrix products, arithmetic and copies ran while one was open for 27% of the time, Pallas kernels for 0%

profile of v1, /device:TPU:1, one launch (start us, length us, event | category | flops | bytes accessed | tf_op | source)
XLA Modules:
  0.0 614.0 jit_solution(7257256603297625840)
XLA Ops:
  7.3 8.0 %fusion.98 = (bf16[1,2048,2,512]{3,2,1,0:T(2,128)(2,1)}, bf16[1,2048,2,512]{3,2,1,0:T(2,128)(2,1)S(1)}) fusion(bf16[2,2048,2,512]{3,2,1,0:T(2,128)(2,1)} %param.20), kind=kLoop, calls=%fused_computation.187 | loop fusion | bytes 16777216 | tf_op jit(solution)/shard_map/slice | solution.py:109
  15.3 3.2 copy.200
  21.5 39.0 %all-gather.4.cloned.1.call-done = bf16[1024,2048]{1,0:T(8,128)(2,1)} async-done(((bf16[1024,512]{1,0:T(8,128)(2,1)}), bf16[1024,2048]{1,0:T(8,128)(2,1)}) %all-gather.4.cloned.1.call-update) | async-done | bytes 4194320 | tf_op jit(solution)/shard_map/all_gather | solution.py:167
  60.5 3.2 fusion.2
  63.9 7.2 %convolution_convert_fusion.3 = bf16[1024,1024]{1,0:T(8,128)(2,1)S(1)} fusion(bf16[2048,1024]{1,0:T(8,128)(2,1)} %bitcast.227, bf16[1024,2048]{1,0:T(8,128)(2,1)S(1)} %copy-done.14, f32[2048]{0:T(1024)S(1)} %bitcast.253, f32[1024]{0:T(1024)S(1)} %add_rsqrt_fusion.1), kind=kOutput, calls=%fused_computation.92 | convolution fusion | flops 4304404480 | bytes 10498048 | tf_op jit(solution)/shard_map/dot_general | solution.py:108
  75.1 23.3 %fusion.107 = f32[8,128,8]{2,0,1:T(8,128)S(1)} fusion(f32[8,128,8]{2,0,1:T(8,128)S(1)} %copy.146), kind=kOutput, calls=%fused_computation.197 | output fusion | flops 1040384 | bytes 65536 | tf_op jit(solution)/shard_map/jit(cumsum)/reduce_window_sum | solution.py:127
  99.0 3.7 collective-permute-start
  102.8 3.5 convolution_convert_fusion.5
  111.1 7.5 %all-to-all-start = ((f32[32,1,8]{2,1,0:T(1,128)}), f32[32,1,8]{2,1,0:T(1,128)S(1)}, u32[]{:S(2)}, u32[]{:S(2)}) async-start(f32[32,1,8]{2,1,0:T(1,128)} %broadcast_in_dim.64), calls=%async_computation | async-start | bytes 32768 | tf_op jit(solution)/shard_map/all_to_all | solution.py:35
  122.8 2.6 divide_multiply_fusion.1
  125.4 2.9 copy.144
  128.3 2.1 copy.201
  132.5 3.5 fusion.43
  137.6 19.8 %while.26 = (s32[]{:T(128)}, f32[8,64,128]{2,1,0:T(8,128)S(1)}, f32[8,8,64,128]{3,2,1,0:T(8,128)}, f32[8,8]{1,0:T(8,128)}, f32[8,8,64,128]{3,2,1,0:T(8,128)}, /*index=5*/s32[]{:T(128)}, s32[]{:T(128)}) while((s32[]{:T(128)}, f32[8,64,128]{2,1,0:T(8,128)S(1)}, f32[8,8,64,128]{3,2,1,0:T(8,128)}, f32[8,8]{1,0:T(8,128)}, ...), condition=%wide.region_3.4_spmd.clone, body=%wide.region_2.3_spmd.clone.sunk | while | flops 262147 | bytes 1311424 | solution.py:139
  157.5 3.1 stack.4
  160.6 7.6 %all-to-all-start.1 = ((bf16[32,1,8,64,128]{4,3,2,1,0:T(8,128)(2,1)}), bf16[32,1,8,64,128]{4,3,2,1,0:T(8,128)(2,1)}, u32[]{:S(2)}, u32[]{:S(2)}) async-start(bf16[32,1,8,64,128]{4,3,2,1,0:T(8,128)(2,1)} %stack.4), calls=%async_computation.1 | async-start | bytes 8388608 | tf_op jit(solution)/shard_map/all_to_all | solution.py:19
  174.5 2.4 reshape.303
  176.9 4.1 copy.159
  183.2 3.1 fusion.110
  186.4 9.6 %fusion.17 = f32[8,8,64,128]{3,2,1,0:T(8,128)} fusion(f32[8,128,8,64]{1,0,3,2:T(8,128)S(1)} %copy-done.18, f32[8,8,128]{2,1,0:T(8,128)S(1)} %copy.147, f32[8,128,128]{2,1,0:T(8,128)S(1)} %fusion.109, pred[128,128]{1,0:T(8,128)(4,1)S(1)} %copy-done.28), kind=kOutput, calls=%fused_computation.30 | convolution fusion | flops 808452096 | bytes 4767744 | tf_op jit(solution)/shard_map/chqk,ckhp->cqhp/dot_general | solution.py:132
  196.0 22.4 %all-to-all-done.1 = bf16[32,1,8,64,128]{4,3,2,1,0:T(8,128)(2,1)} async-done(((bf16[32,1,8,64,128]{4,3,2,1,0:T(8,128)(2,1)}), bf16[32,1,8,64,128]{4,3,2,1,0:T(8,128)(2,1)}, u32[]{:S(2)}, u32[]{:S(2)}) %all-to-all-start.1) | async-done | bytes 4194336 | tf_op jit(solution)/shard_map/all_to_all | solution.py:19
  218.4 6.2 %fusion.10 = f32[8,1,64,128]{3,1,2,0:T(1,128)S(1)} fusion(f32[32,8,1,1]{0,2,3,1:T(1,128)S(1)} %copy.184, bf16[32,8,64,128]{3,2,1,0:T(8,128)(2,1)} %bitcast.29), kind=kOutput, calls=%fused_computation.23 | convolution fusion | flops 25165824 | bytes 4457472 | tf_op jit(solution)/shard_map/mh,mhpn->hpn/dot_general | solution.py:91
  224.7 5.1 fusion.42
  229.8 2.8 copy.192
  232.6 4.8 reshape.301
  239.6 8.5 %convolution_convert_fusion.1 = bf16[1024,2048]{1,0:T(8,128)(2,1)} fusion(bf16[2,512,2048]{2,1,0:T(8,128)(2,1)} %param.29, f32[1024,512]{1,0:T(8,128)} %copy.160, f32[1024,512]{1,0:T(8,128)} %reshape.301, f32[1024,512]{1,0:T(8,128)} %divide_multiply_fusion.1, f32[512]{0:T(512)S(1)} %bitcast.265, f32[512]{0:T(512)S(1)} %copy-done.45, ...), kind=kOutput, calls=%fused_computation.36 | convolution fusion | flops 2155347968 | bytes 13635584 | tf_op jit(solution)/shard_map/dot_general | solution.py:163
  248.8 4.4 sort.34
  253.1 4.5 gather_fusion
  259.1 6.9 %all_to_all.48 = s32[2,1,512]{2,1,0:T(1,128)S(1)} all-to-all(s32[2,1,512]{2,1,0:T(1,128)S(1)} %reshape.314), channel_id=1, replica_groups=mesh['seq_0'=4,'seq_1'=4,'seq_2'=2,'tp'=4] {'seq_2'}, dimensions={0} | all-to-all | bytes 8192 | tf_op jit(solution)/shard_map/all_to_all | solution.py:58
  266.7 9.0 %all_to_all.49 = s32[16,2,1,32]{3,2,1,0:T(1,128)S(1)} all-to-all(s32[16,2,1,32]{3,2,1,0:T(1,128)S(1)} %copy.162), channel_id=1, replica_groups=mesh['seq_0'=4,'seq_1'=4,'seq_2'=2,'tp'=4] {'seq_0','seq_1'}, dimensions={0} | all-to-all | bytes 8192 | tf_op jit(solution)/shard_map/all_to_all | solution.py:58
  277.1 16.8 %reduce-scatter.3.cloned.1.call-done = bf16[1024,512]{1,0:T(8,128)(2,1)} async-done(((bf16[1024,2048]{1,0:T(8,128)(2,1)}), bf16[1024,512]{1,0:T(8,128)(2,1)}) %reduce-scatter.3.cloned.1.call-update) | async-done | bytes 1048592 | tf_op jit(solution)/shard_map/reduce_scatter | solution.py:171
  295.4 4.0 gather_fusion.1
  299.5 4.8 all_to_all.50
  305.4 6.7 %all-to-all-start.5 = ((bf16[16,2,1,32,512]{4,3,1,2,0:T(8,128)(2,1)}), bf16[16,2,1,32,512]{4,3,1,2,0:T(8,128)(2,1)S(1)}, u32[]{:S(2)}, u32[]{:S(2)}) async-start(bf16[16,2,1,32,512]{4,3,1,2,0:T(8,128)(2,1)} %copy.164), calls=%async_computation.6 | async-start | bytes 2097152 | tf_op jit(solution)/shard_map/all_to_all | solution.py:58
  312.1 4.4 sort.35
  316.5 11.9 %all-to-all-done.5 = bf16[16,2,1,32,512]{4,3,1,2,0:T(8,128)(2,1)S(1)} async-done(((bf16[16,2,1,32,512]{4,3,1,2,0:T(8,128)(2,1)}), bf16[16,2,1,32,512]{4,3,1,2,0:T(8,128)(2,1)S(1)}, u32[]{:S(2)}, u32[]{:S(2)}) %all-to-all-start.5) | async-done | bytes 1048608 | tf_op jit(solution)/shard_map/all_to_all | solution.py:58
  328.4 5.2 gather_fusion.2
  333.7 5.4 copy.202
  339.0 40.3 %all-gather.6.cloned.1.call-done = bf16[1024,2048]{1,0:T(8,128)(2,1)} async-done(((bf16[1024,512]{1,0:T(8,128)(2,1)}), bf16[1024,2048]{1,0:T(8,128)(2,1)}) %all-gather.6.cloned.1.call-update) | async-done | bytes 4194320 | tf_op jit(solution)/shard_map/all_gather | solution.py:167
  379.4 3.2 fusion.5
  382.8 7.2 %convolution_convert_fusion.2 = bf16[1024,1024]{1,0:T(8,128)(2,1)S(1)} fusion(bf16[2048,1024]{1,0:T(8,128)(2,1)} %bitcast.228, bf16[1024,2048]{1,0:T(8,128)(2,1)S(1)} %copy-done.15, f32[2048]{0:T(1024)S(1)} %bitcast.250, f32[1024]{0:T(1024)S(1)} %add_rsqrt_fusion), kind=kOutput, calls=%fused_computation.91 | convolution fusion | flops 4304404480 | bytes 10498048 | tf_op jit(solution)/shard_map/dot_general | solution.py:108
  393.4 23.3 %fusion.108 = f32[8,128,8]{2,0,1:T(8,128)S(1)} fusion(f32[8,128,8]{2,0,1:T(8,128)S(1)} %copy.167), kind=kOutput, calls=%fused_computation.198 | output fusion | flops 1040384 | bytes 65536 | tf_op jit(solution)/shard_map/jit(cumsum)/reduce_window_sum | solution.py:127
  416.7 3.8 convolution_convert_fusion.4
  421.3 3.7 collective-permute-start.3
  428.5 7.6 %all-to-all-start.6 = ((f32[32,1,8]{2,1,0:T(1,128)}), f32[32,1,8]{2,1,0:T(1,128)S(1)}, u32[]{:S(2)}, u32[]{:S(2)}) async-start(f32[32,1,8]{2,1,0:T(1,128)} %broadcast_in_dim.112), calls=%async_computation.7 | async-start | bytes 32768 | tf_op jit(solution)/shard_map/all_to_all | solution.py:35
  439.7 2.5 divide_multiply_fusion
  442.2 2.9 copy.165
  445.1 2.1 copy.203
  449.2 3.5 fusion.36
  454.4 14.4 %while.27 = (s32[]{:T(128)}, f32[8,64,128]{2,1,0:T(8,128)S(1)}, f32[8,8,64,128]{3,2,1,0:T(8,128)}, f32[8,8]{1,0:T(8,128)S(1)}, f32[8,8,64,128]{3,2,1,0:T(8,128)}, /*index=5*/s32[]{:T(128)}, s32[]{:T(128)}) while((s32[]{:T(128)}, f32[8,64,128]{2,1,0:T(8,128)S(1)}, f32[8,8,64,128]{3,2,1,0:T(8,128)}, f32[8,8]{1,0:T(8,128)S(1)}, ...), condition=%wide.region_15.16_spmd.clone, body=%wide.region_14.15_spmd.clone.sunk | while | flops 262147 | bytes 1311424 | solution.py:139
  468.8 3.1 stack.5
  471.9 7.6 %all-to-all-start.7 = ((bf16[32,1,8,64,128]{4,3,2,1,0:T(8,128)(2,1)}), bf16[32,1,8,64,128]{4,3,2,1,0:T(8,128)(2,1)}, u32[]{:S(2)}, u32[]{:S(2)}) async-start(bf16[32,1,8,64,128]{4,3,2,1,0:T(8,128)(2,1)} %stack.5), calls=%async_computation.8 | async-start | bytes 8388608 | tf_op jit(solution)/shard_map/all_to_all | solution.py:19
  484.1 2.4 reshape.304
  486.5 4.3 copy.180
  492.4 3.2 fusion.112
  495.6 9.7 %fusion.12 = f32[8,8,64,128]{3,2,1,0:T(8,128)} fusion(f32[8,128,8,64]{1,0,3,2:T(8,128)S(1)} %copy-done.19, f32[8,8,128]{2,1,0:T(8,128)S(1)} %copy.168, f32[8,128,128]{2,1,0:T(8,128)S(1)} %fusion.111, pred[128,128]{1,0:T(8,128)(4,1)S(1)} %copy-done.29), kind=kOutput, calls=%fused_computation.25 | convolution fusion | flops 808452096 | bytes 4767744 | tf_op jit(solution)/shard_map/chqk,ckhp->cqhp/dot_general | solution.py:132
  505.3 24.5 %all-to-all-done.7 = bf16[32,1,8,64,128]{4,3,2,1,0:T(8,128)(2,1)} async-done(((bf16[32,1,8,64,128]{4,3,2,1,0:T(8,128)(2,1)}), bf16[32,1,8,64,128]{4,3,2,1,0:T(8,128)(2,1)}, u32[]{:S(2)}, u32[]{:S(2)}) %all-to-all-start.7) | async-done | bytes 4194336 | tf_op jit(solution)/shard_map/all_to_all | solution.py:19
  529.7 6.0 fusion.8
  535.8 5.1 fusion.35
  540.9 2.7 copy.193
  543.7 4.8 reshape.302
  550.7 8.5 %convolution_convert_fusion = bf16[1024,2048]{1,0:T(8,128)(2,1)} fusion(bf16[2,512,2048]{2,1,0:T(8,128)(2,1)} %param.29, f32[1024,512]{1,0:T(8,128)} %copy.181, f32[1024,512]{1,0:T(8,128)} %reshape.302, f32[1024,512]{1,0:T(8,128)} %divide_multiply_fusion, f32[512]{0:T(512)S(1)} %bitcast.264, f32[512]{0:T(512)S(1)} %copy-done.46, ...), kind=kOutput, calls=%fused_computation.35 | convolution fusion | flops 2155347968 | bytes 13635584 | tf_op jit(solution)/shard_map/dot_general | solution.py:163
  559.1 45.7 %reduce-scatter.5.cloned.1.call-done = bf16[1024,512]{1,0:T(8,128)(2,1)} async-done(((bf16[1024,2048]{1,0:T(8,128)(2,1)}), bf16[1024,512]{1,0:T(8,128)(2,1)}) %reduce-scatter.5.cloned.1.call-update) | async-done | bytes 1048592 | tf_op jit(solution)/shard_map/reduce_scatter | solution.py:171
  604.8 2.5 add_convert_fusion
  (290 shorter events, 95.8 us)
Async XLA Ops:
  6.5 53.9 %all-gather.4.cloned.1.call-start = ((), (), s32[]{:S(2)}) async-start(), calls=%async_computation.10 | async-start | bytes 5242880 | tf_op jit(solution)/shard_map/all_gather | solution.py:167
  15.2 3.2 copy-start.53
  15.2 3.8 copy-start.54
  15.2 4.4 copy-start.36
  15.2 5.0 copy-start.26
  15.3 5.6 copy-start.27
  60.5 3.4 copy-start.14
  71.1 1.7 copy-start.16
  71.1 2.3 copy-start.58
  75.1 27.7 %copy-start.57 = (bf16[2,2048,256]{2,1,0:T(8,128)(2,1)S(1)}, bf16[2,2048,256]{2,1,0:T(8,128)(2,1)}, u32[]{:S(2)}) copy-start(bf16[2,2048,256]{2,1,0:T(8,128)(2,1)} %param.21) | copy-start | bytes 6291460
  99.0 23.0 %collective-permute-start = (bf16[3,512]{1,0:T(4,128)(2,1)}, bf16[3,512]{1,0:T(4,128)(2,1)S(1)}, u32[]{:S(2)}, u32[]{:S(2)}) collective-permute-start(bf16[3,512]{1,0:T(4,128)(2,1)} %slice.314), channel_id=1, source_target_pairs={{0,4},{4,8},{8,12},{12,16},{16,20},{20,24},{24,28},{28,32},{32,36}... | collective-permute-start | bytes 9224 | tf_op jit(solution)/shard_map/ppermute | solution.py:45
  107.7 10.9 %collective-permute-start.1 = (bf16[3,256]{1,0:T(4,128)(2,1)}, bf16[3,256]{1,0:T(4,128)(2,1)}, u32[]{:S(2)}, u32[]{:S(2)}) collective-permute-start(bf16[3,256]{1,0:T(4,128)(2,1)} %slice.320), channel_id=1, source_target_pairs={{0,4},{4,8},{8,12},{12,16},{16,20},{20,24},{24,28},{28,32},{32,36}... | collective-permute-start | bytes 4616 | tf_op jit(solution)/shard_map/ppermute | solution.py:45
  111.1 46.4 %all-to-all-start = ((f32[32,1,8]{2,1,0:T(1,128)}), f32[32,1,8]{2,1,0:T(1,128)S(1)}, u32[]{:S(2)}, u32[]{:S(2)}) async-start(f32[32,1,8]{2,1,0:T(1,128)} %broadcast_in_dim.64), calls=%async_computation | async-start | bytes 32768 | tf_op jit(solution)/shard_map/all_to_all | solution.py:35
  121.1 1.4 copy-start.13
  130.4 2.1 copy-start.1
  130.4 2.1 copy-start.7
  160.5 7.6 %copy-start.55 = (f32[2,8]{1,0:T(2,128)S(1)}, f32[2,8]{1,0:T(2,128)}, u32[]{:S(2)}) copy-start(f32[2,8]{1,0:T(2,128)} %param.27) | copy-start | bytes 196
  160.6 9.6 %copy-start.43 = (f32[2,512]{1,0:T(2,128)S(1)}, f32[2,512]{1,0:T(2,128)}, u32[]{:S(2)}) copy-start(f32[2,512]{1,0:T(2,128)} %param.28) | copy-start | bytes 12292
  160.6 10.4 %copy-start.24 = (f32[8,8]{1,0:T(8,128)S(1)}, f32[8,8]{1,0:T(8,128)}, u32[]{:S(2)}) copy-start(f32[8,8]{1,0:T(8,128)} %get-tuple-element.145) | copy-start | bytes 772
  160.6 57.8 %all-to-all-start.1 = ((bf16[32,1,8,64,128]{4,3,2,1,0:T(8,128)(2,1)}), bf16[32,1,8,64,128]{4,3,2,1,0:T(8,128)(2,1)}, u32[]{:S(2)}, u32[]{:S(2)}) async-start(bf16[32,1,8,64,128]{4,3,2,1,0:T(8,128)(2,1)} %stack.4), calls=%async_computation.1 | async-start | bytes 8388608 | tf_op jit(solution)/shard_map/all_to_all | solution.py:19
  168.1 125.8 %reduce-scatter.3.cloned.1.call-start = ((), (), s32[]{:S(2)}) async-start(), calls=%async_computation.11 | async-start | bytes 5242880 | tf_op jit(solution)/shard_map/reduce_scatter | solution.py:171
  168.8 8.1 %copy-start.49 = (f32[8]{0:T(128)}, f32[8]{0:T(128)S(1)}, u32[]{:S(2)}) copy-start(f32[8]{0:T(128)S(1)} %get-tuple-element.170) | copy-start | bytes 100
  169.5 11.6 %copy-start.34 = (pred[32]{0:T(512)(128)(4,1)}, pred[32]{0:T(512)(128)(4,1)S(1)}, u32[]{:S(2)}) copy-start(pred[32]{0:T(512)(128)(4,1)S(1)} %iota_compare_fusion.1) | copy-start | bytes 100
  176.9 5.1 copy-start.8
  176.9 6.3 %copy-start.5 = (f32[8,8,64,128]{3,2,1,0:T(8,128)S(1)}, f32[8,8,64,128]{3,2,1,0:T(8,128)}, u32[]{:S(2)}) copy-start(f32[8,8,64,128]{3,2,1,0:T(8,128)} %get-tuple-element.63) | copy-start | bytes 6291460
  183.2 3.2 copy-start.18
  183.2 3.2 copy-start.28
  218.4 6.3 %copy-start.2 = (f32[64,8,8,128]{3,2,1,0:T(8,128)S(1)}, f32[64,8,8,128]{3,2,1,0:T(8,128)}, u32[]{:S(2)}) copy-start(f32[64,8,8,128]{3,2,1,0:T(8,128)} %copy-done.1) | copy-start | bytes 6291460
  218.4 6.3 %copy-start.21 = (f32[8,128,8,64]{1,3,2,0:T(8,128)S(1)}, f32[8,128,8,64]{1,3,2,0:T(8,128)}, u32[]{:S(2)}) copy-start(f32[8,128,8,64]{1,3,2,0:T(8,128)} %copy.159) | copy-start | bytes 6291460
  218.4 6.3 %copy-start.50 = (f32[8]{0:T(128)S(1)}, f32[8]{0:T(128)}, u32[]{:S(2)}) copy-start(f32[8]{0:T(128)} %copy-done.49) | copy-start | bytes 100
  237.7 1.9 copy-start.45
  237.7 1.9 copy-start.52
  253.1 40.8 %copy-start.11 = (bf16[1024,512]{1,0:T(8,128)(2,1)S(1)}, bf16[1024,512]{1,0:T(8,128)(2,1)}, u32[]{:S(2)}) copy-start(bf16[1024,512]{1,0:T(8,128)(2,1)} %param.17) | copy-start | bytes 3145732
  305.4 23.0 %all-to-all-start.5 = ((bf16[16,2,1,32,512]{4,3,1,2,0:T(8,128)(2,1)}), bf16[16,2,1,32,512]{4,3,1,2,0:T(8,128)(2,1)S(1)}, u32[]{:S(2)}, u32[]{:S(2)}) async-start(bf16[16,2,1,32,512]{4,3,1,2,0:T(8,128)(2,1)} %copy.164), calls=%async_computation.6 | async-start | bytes 2097152 | tf_op jit(solution)/shard_map/all_to_all | solution.py:58
  312.1 67.3 %all-gather.6.cloned.1.call-start = ((), (), s32[]{:S(2)}) async-start(), calls=%async_computation.13 | async-start | bytes 5242880 | tf_op jit(solution)/shard_map/all_gather | solution.py:167
  339.0 43.6 %copy-start.37 = (f32[1,2048]{1,0:T(1,128)S(1)}, f32[1,2048]{1,0:T(1,128)}, u32[]{:S(2)}) copy-start(f32[1,2048]{1,0:T(1,128)} %get-tuple-element.155) | copy-start | bytes 24580
  379.4 3.4 copy-start.15
  390.0 1.7 copy-start.17
  390.0 1.7 copy-start.56
  390.1 1.7 copy-start.59
  420.6 16.7 %copy-start.38 = (f32[1,1,256]{2,1,0:T(1,128)S(1)}, f32[1,1,256]{2,1,0:T(1,128)}, u32[]{:S(2)}) copy-start(f32[1,1,256]{2,1,0:T(1,128)} %get-tuple-element.157) | copy-start | bytes 3076
  420.6 16.7 %copy-start.39 = (f32[1,1,256]{2,1,0:T(1,128)S(1)}, f32[1,1,256]{2,1,0:T(1,128)}, u32[]{:S(2)}) copy-start(f32[1,1,256]{2,1,0:T(1,128)} %get-tuple-element.158) | copy-start | bytes 3076
  420.6 16.7 %copy-start.40 = (f32[1,1,256]{2,1,0:T(1,128)S(1)}, f32[1,1,256]{2,1,0:T(1,128)}, u32[]{:S(2)}) copy-start(f32[1,1,256]{2,1,0:T(1,128)} %get-tuple-element.163) | copy-start | bytes 3076
  420.6 16.7 %copy-start.41 = (f32[1,1,256]{2,1,0:T(1,128)S(1)}, f32[1,1,256]{2,1,0:T(1,128)}, u32[]{:S(2)}) copy-start(f32[1,1,256]{2,1,0:T(1,128)} %get-tuple-element.164) | copy-start | bytes 3076
  421.3 14.8 %collective-permute-start.3 = (bf16[3,256]{1,0:T(4,128)(2,1)}, bf16[3,256]{1,0:T(4,128)(2,1)S(1)}, u32[]{:S(2)}, u32[]{:S(2)}) collective-permute-start(bf16[3,256]{1,0:T(4,128)(2,1)} %slice.336), channel_id=1, source_target_pairs={{0,4},{4,8},{8,12},{12,16},{16,20},{20,24},{24,28},{28,32},{32,36}... | collective-permute-start | bytes 4616 | tf_op jit(solution)/shard_map/ppermute | solution.py:45
  425.4 13.5 %collective-permute-start.2 = (bf16[3,512]{1,0:T(4,128)(2,1)S(1)}, bf16[3,512]{1,0:T(4,128)(2,1)S(1)}, u32[]{:S(2)}, u32[]{:S(2)}) collective-permute-start(bf16[3,512]{1,0:T(4,128)(2,1)S(1)} %slice.330), channel_id=1, source_target_pairs={{0,4},{4,8},{8,12},{12,16},{16,20},{20,24},{24,28},{28,32},{32,36}... | collective-permute-start | bytes 9224 | tf_op jit(solution)/shard_map/ppermute | solution.py:45
  428.5 40.3 %all-to-all-start.6 = ((f32[32,1,8]{2,1,0:T(1,128)}), f32[32,1,8]{2,1,0:T(1,128)S(1)}, u32[]{:S(2)}, u32[]{:S(2)}) async-start(f32[32,1,8]{2,1,0:T(1,128)} %broadcast_in_dim.112), calls=%async_computation.7 | async-start | bytes 32768 | tf_op jit(solution)/shard_map/all_to_all | solution.py:35
  447.2 2.0 copy-start.3
  447.2 2.0 copy-start.9
  471.9 7.6 %copy-start.47 = (f32[8]{0:T(128)S(1)}, f32[8]{0:T(128)}, u32[]{:S(2)}) copy-start(f32[8]{0:T(128)} %get-tuple-element.169) | copy-start | bytes 100
  471.9 8.5 %copy-start.25 = (f32[8,8]{1,0:T(8,128)S(1)}, f32[8,8]{1,0:T(8,128)}, u32[]{:S(2)}) copy-start(f32[8,8]{1,0:T(8,128)} %get-tuple-element.141) | copy-start | bytes 772
  471.9 57.8 %all-to-all-start.7 = ((bf16[32,1,8,64,128]{4,3,2,1,0:T(8,128)(2,1)}), bf16[32,1,8,64,128]{4,3,2,1,0:T(8,128)(2,1)}, u32[]{:S(2)}, u32[]{:S(2)}) async-start(bf16[32,1,8,64,128]{4,3,2,1,0:T(8,128)(2,1)} %stack.5), calls=%async_computation.8 | async-start | bytes 8388608 | tf_op jit(solution)/shard_map/all_to_all | solution.py:19
  479.5 125.3 %reduce-scatter.5.cloned.1.call-start = ((), (), s32[]{:S(2)}) async-start(), calls=%async_computation.12 | async-start | bytes 5242880 | tf_op jit(solution)/shard_map/reduce_scatter | solution.py:171
  486.5 4.4 copy-start.35
  486.5 4.7 copy-start.10
  486.5 5.9 copy-start.6
  492.4 3.2 copy-start.19
  492.4 3.2 copy-start.29
  529.7 6.0 copy-start.4
  529.7 6.0 copy-start.20
  529.7 6.0 copy-start.48
  548.7 2.0 copy-start.46
  548.7 1.9 copy-start.51
  559.1 45.7 %copy-start = (bf16[1024,512]{1,0:T(8,128)(2,1)S(1)}, bf16[1024,512]{1,0:T(8,128)(2,1)}, u32[]{:S(2)}) copy-start(bf16[1024,512]{1,0:T(8,128)(2,1)} %gather_fusion.2) | copy-start | bytes 3145732
  (9 other events, 8.4 us)
Sparse Core Ops, SparseCore 0:
  9.0 51.3 all-gather.3
  248.2 45.6 reduce-scatter.2
  333.8 45.5 all-gather.5
  559.3 45.4 reduce-scatter.4
